TPU v7x, 512 devices: a whole 4x4x16 slice. The times are simulated.
512 devices in a mesh: tgt: 16 (over y, x_lo, core), src: 32 (over z, x_hi).
Axes of the slice: x: 4 (x_hi: 2, x_lo: 2; x = x_hi * 2 + x_lo), y: 4, z: 16, core: 2. Of those that a mesh axis runs over, the one named last changes fastest.
Arguments:
- shear_leaves: bfloat16 [32, 32, 128, 128], P('tgt', 'src'), may hold values from -2 to 2, as said below
- normal_leaves: bfloat16 [32, 32, 128, 128], P('tgt', 'src'), may hold values from -2 to 2, as said below
- near_flags: int32 [32, 32], P('tgt', 'src'), may hold values from 0 to 1, as said below
- ranks: int32 [32, 32], P('tgt', 'src'), may hold values from 16 to 64
- shear_traction: float32 [4096, 128], P(('tgt', 'src')), may hold values from -1 to 1
- normal_traction: float32 [4096, 128], P(('tgt', 'src')), may hold values from 0.5 to 4
- state: float32 [4096, 128], P(('tgt', 'src')), may hold values from -0.5 to 0.5
- friction_a: float32 [4096, 128], P(('tgt', 'src')), may hold values from 1 to 2
- heal_rate: float32 [4096, 128], P(('tgt', 'src')), may hold values from 0.1 to 0.5
Outputs:
- shear_out: float32 [4096, 128], P(('tgt', 'src'))
- normal_out: float32 [4096, 128], P(('tgt', 'src'))
- state_out: float32 [4096, 128], P(('tgt', 'src'))
Inputs may be any that keep to these rules, and one draw needn't show every extreme that they name: `near_flags`: every leaf with equal leaf row and leaf column is 1, and a 1 stands only where the leaf row and the leaf column differ by at most 1. `shear_leaves`: columns 0 to 63 of an admissible leaf hold its factor U, columns 64 onward its factor V. `normal_leaves`: columns 0 to 63 of an admissible leaf hold its factor U, columns 64 onward its factor V.
All inputs are finite; a program needn't handle non-finite values.
Results may differ from a plain program's by a relative error of at most 0.002.
Values may be sent and summed in bfloat16 or wider, within the bound.
A program may use at most 64 MiB of HBM per device.

v0:
```python
import jax
import jax.numpy as jnp
from jax import lax
from jax.sharding import PartitionSpec as P

RMAX = 64
BLK = 128
time_step = 0.25


def spread(block, axis, owner):
    block = jnp.where(lax.axis_index(axis) == owner, block, jnp.zeros_like(block))
    return lax.psum(block, axis)


def kernel_terms(leaves, near_flags, ranks, source):
    leaf_rows, leaf_cols = near_flags.shape
    members = source.shape[-1]
    blocks = source.reshape(leaf_cols, BLK, members)
    factor_u = leaves[:, :, :, :RMAX]
    factor_v = leaves[:, :, :, RMAX:]
    inner = jnp.einsum("rcjk,cjn->rckn", factor_v, blocks, preferred_element_type=jnp.float32)
    keep_mask = (jnp.arange(RMAX, dtype=jnp.int32)[None, None, :] < ranks[:, :, None]) & (
        near_flags[:, :, None] == 0
    )
    inner = jnp.where(keep_mask[:, :, :, None], inner, 0.0).astype(jnp.bfloat16)
    lowrank = jnp.einsum("rcik,rckn->rin", factor_u, inner, preferred_element_type=jnp.float32)
    masked = jnp.where((near_flags == 1)[:, :, None, None], leaves, jnp.zeros((), leaves.dtype))
    dense_sum = jnp.einsum("rcij,cjn->rin", masked, blocks, preferred_element_type=jnp.float32)
    return (lowrank + dense_sum).reshape(leaf_rows * BLK, members)


def to_source(block_rows, leaf_rows, leaf_cols, src_index):
    first_leaf = src_index * leaf_cols
    offset = first_leaf % leaf_rows * BLK
    owner = first_leaf // leaf_rows
    piece = lax.dynamic_slice_in_dim(block_rows, offset, leaf_cols * BLK, 0)
    return spread(piece, "tgt", owner)


def friction(shear_now, normal_now, state_now, friction_a):
    effective = jnp.maximum(normal_now, 1.0)
    slip_rate = (
        2.0 * jnp.exp(-state_now / friction_a) * jnp.sinh(shear_now / (friction_a * effective))
    )
    return (slip_rate, (slip_rate - 1.0).astype(jnp.bfloat16))


def advance(rates, start):
    first_rates = rates(*start)
    first = tuple((value + time_step * change for value, change in zip(start, first_rates)))
    second_rates = rates(*first)
    second = tuple(
        (
            0.75 * begin + 0.25 * (value + time_step * change)
            for begin, value, change in zip(start, first, second_rates)
        )
    )
    third_rates = rates(*second)
    return tuple(
        (
            begin / 3.0 + 2.0 / 3.0 * (value + time_step * change)
            for begin, value, change in zip(start, second, third_rates)
        )
    )


def per_device(
    shear_leaves,
    normal_leaves,
    near_flags,
    ranks,
    shear_traction,
    normal_traction,
    state,
    friction_a,
    heal_rate,
):
    leaf_rows, leaf_cols = near_flags.shape
    src_index = lax.axis_index("src")

    def both_kernels(block_rows):
        source = to_source(block_rows, leaf_rows, leaf_cols, src_index)
        shear_part = kernel_terms(shear_leaves, near_flags, ranks, source)
        normal_part = kernel_terms(normal_leaves, near_flags, ranks, source)
        return (shear_part, normal_part)

    def own_rates(shear_now, normal_now, state_now):
        slip_rate, deviation = friction(shear_now, normal_now, state_now, friction_a)
        block_rows = lax.all_gather(deviation, "src", axis=0, tiled=True)
        shear_part, normal_part = both_kernels(block_rows)
        shear_rate, normal_rate = (
            lax.psum_scatter(shear_part, "src", scatter_dimension=0, tiled=True),
            lax.psum_scatter(normal_part, "src", scatter_dimension=0, tiled=True),
        )
        return (shear_rate, normal_rate, heal_rate * (jnp.exp(-state_now) - slip_rate))

    outputs = advance(own_rates, (shear_traction, normal_traction, state))
    return (outputs[0], outputs[1], outputs[2])


def solution(mesh):
    in_specs = (
        P("tgt", "src", None, None),
        P("tgt", "src", None, None),
        P("tgt", "src"),
        P("tgt", "src"),
        P(("tgt", "src"), None),
        P(("tgt", "src"), None),
        P(("tgt", "src"), None),
        P(("tgt", "src"), None),
        P(("tgt", "src"), None),
    )
    out_specs = (P(("tgt", "src"), None), P(("tgt", "src"), None), P(("tgt", "src"), None))
    return jax.shard_map(
        per_device, mesh=mesh, in_specs=in_specs, out_specs=out_specs, check_vma=False
    )
```

profile of v0, /device:TPU:8, one launch (start us, length us, event | category | flops | bytes accessed | tf_op | source)
XLA Modules:
  0.0 1324.7 jit_solution(18217465613332605597)
XLA Ops:
  7.2 0.0 all-reduce.17.cloned.1.call-start
  7.3 0.6 copy-done.7
  7.9 0.0 copy-done.4
  7.9 0.0 copy-done.3
  8.0 0.0 copy-done.2
  8.0 82.7 %all_gather.9 = bf16[256,128]{1,0:T(8,128)(2,1)S(1)} all-gather(bf16[8,128]{1,0:T(8,128)(2,1)S(1)} %get-tuple-element.13), channel_id=1, replica_groups=mesh['tgt'=16,'src'=32] {'src'}, dimensions={0}, use_global_device_ids=true | all-gather | bytes 67584 | tf_op jit(solution)/shard_map/all_gather | solution.py:90
  90.7 46.2 %psum.21 = bf16[128,128]{1,0:T(8,128)(2,1)S(1)} all-reduce(bf16[128,128]{1,0:T(8,128)(2,1)S(1)} %dynamic-slice_select_fusion.2), channel_id=1, replica_groups=mesh['tgt'=16,'src'=32] {'tgt'}, use_global_device_ids=true, to_apply=%region_0.1 | all-reduce | flops 16384 | bytes 65536 | tf_op jit(solution)/shard_map/psum | solution.py:13
  136.9 0.1 slice.8
  137.0 0.7 copy-done
  137.8 0.1 slice.10
  137.9 0.2 fusion.16
  138.1 0.2 fusion.22
  138.3 0.1 copy.20
  138.4 0.1 fusion.93
  138.5 0.1 copy.22
  138.6 0.1 fusion.94
  138.8 0.7 copy-done.8
  139.4 0.1 compare_and_fusion
  139.5 0.9 fusion.1
  140.4 0.9 fusion
  141.2 0.0 all-reduce.17.cloned.1.call-update
  141.3 0.0 all-reduce.15.cloned.1.call-start
  141.3 1.3 dynamic-slice
  143.3 306.4 %all-reduce.17.cloned.1.call-done = (f32[256,128]{1,0:T(8,128)}, f32[256,128]{1,0:T(8,128)}) async-done(((f32[256,128]{1,0:T(8,128)}, f32[256,128]{1,0:T(8,128)}), (f32[256,128]{1,0:T(8,128)}, f32[256,128]{1,0:T(8,128)})) %all-reduce.17.cloned.1.call-update) | async-done | bytes 262160
  449.6 0.7 add_convert_fusion.1
  450.3 73.7 %all_gather.10 = bf16[256,128]{1,0:T(8,128)(2,1)S(1)} all-gather(bf16[8,128]{1,0:T(8,128)(2,1)S(1)} %get-tuple-element.11), channel_id=1, replica_groups=mesh['tgt'=16,'src'=32] {'src'}, dimensions={0}, use_global_device_ids=true | all-gather | bytes 67584 | tf_op jit(solution)/shard_map/all_gather | solution.py:90
  524.1 46.2 %psum.22 = bf16[128,128]{1,0:T(8,128)(2,1)S(1)} all-reduce(bf16[128,128]{1,0:T(8,128)(2,1)S(1)} %dynamic-slice_select_fusion.1), channel_id=1, replica_groups=mesh['tgt'=16,'src'=32] {'tgt'}, use_global_device_ids=true, to_apply=%region_3.4 | all-reduce | flops 16384 | bytes 65536 | tf_op jit(solution)/shard_map/psum | solution.py:13
  570.3 0.1 fusion.95
  570.4 0.1 fusion.96
  570.5 0.2 fusion.14
  570.7 0.2 fusion.20
  570.9 0.9 fusion.3
  571.8 0.9 fusion.2
  572.7 0.0 all-reduce.15.cloned.1.call-update
  572.7 0.0 all-reduce.13.cloned.1.call-start
  572.8 310.1 %all-reduce.15.cloned.1.call-done = (f32[256,128]{1,0:T(8,128)}, f32[256,128]{1,0:T(8,128)}) async-done(((f32[256,128]{1,0:T(8,128)}, f32[256,128]{1,0:T(8,128)}), (f32[256,128]{1,0:T(8,128)}, f32[256,128]{1,0:T(8,128)})) %all-reduce.15.cloned.1.call-update) | async-done | bytes 262160
  882.9 1.3 multiply_add_fusion
  884.3 73.7 %all_gather.11 = bf16[256,128]{1,0:T(8,128)(2,1)S(1)} all-gather(bf16[8,128]{1,0:T(8,128)(2,1)S(1)} %add_convert_fusion), channel_id=1, replica_groups=mesh['tgt'=16,'src'=32] {'src'}, dimensions={0}, use_global_device_ids=true | all-gather | bytes 67584 | tf_op jit(solution)/shard_map/all_gather | solution.py:90
  958.0 46.2 %psum.23 = bf16[128,128]{1,0:T(8,128)(2,1)S(1)} all-reduce(bf16[128,128]{1,0:T(8,128)(2,1)S(1)} %dynamic-slice_select_fusion), channel_id=1, replica_groups=mesh['tgt'=16,'src'=32] {'tgt'}, use_global_device_ids=true, to_apply=%region_6.7 | all-reduce | flops 16384 | bytes 65536 | tf_op jit(solution)/shard_map/psum | solution.py:13
  1004.1 0.1 fusion.97
  1004.3 0.1 fusion.98
  1004.4 0.2 fusion.12
  1004.6 0.2 fusion.18
  1004.8 0.9 fusion.5
  1005.7 0.9 fusion.4
  1006.6 0.0 all-reduce.13.cloned.1.call-update
  1006.6 310.2 %all-reduce.13.cloned.1.call-done = (f32[256,128]{1,0:T(8,128)}, f32[256,128]{1,0:T(8,128)}) async-done(((f32[256,128]{1,0:T(8,128)}, f32[256,128]{1,0:T(8,128)}), (f32[256,128]{1,0:T(8,128)}, f32[256,128]{1,0:T(8,128)})) %all-reduce.13.cloned.1.call-update) | async-done | bytes 262160
  1316.8 1.4 fusion.71
  (18 shorter events, 0.1 us)
Async XLA Ops:
  7.2 442.5 %all-reduce.17.cloned.1.call-start = ((), (), s32[]{:S(2)}) async-start(), calls=%async_computation.2 | async-start | bytes 524288
  7.2 0.7 copy-start.5
  7.2 0.7 copy-start.4
  7.2 0.7 copy-start.7
  7.3 0.7 copy-start.3
  7.3 0.7 copy-start.2
  90.7 46.2 %copy-start.1 = (bf16[2,1,128,128]{3,2,1,0:T(8,128)(2,1)S(1)}, bf16[2,1,128,128]{3,2,1,0:T(8,128)(2,1)}, u32[]{:S(2)}) copy-start(bf16[2,1,128,128]{3,2,1,0:T(8,128)(2,1)} %param.9) | copy-start | bytes 196612
  136.9 0.8 copy-start
  138.8 0.7 copy-start.8
  141.3 741.6 %all-reduce.15.cloned.1.call-start = ((), (), s32[]{:S(2)}) async-start(), calls=%async_computation.1 | async-start | bytes 524288
  143.2 306.4 %copy-start.6 = (f32[8,128]{1,0:T(8,128)S(1)}, f32[8,128]{1,0:T(8,128)}, u32[]{:S(2)}) copy-start(f32[8,128]{1,0:T(8,128)} %param.17) | copy-start | bytes 12292
  572.7 744.1 %all-reduce.13.cloned.1.call-start = ((), (), s32[]{:S(2)}) async-start(), calls=%async_computation | async-start | bytes 524288
Sparse Core Ops, SparseCore 0:
  141.4 308.1 all-reduce.16
  572.8 310.0 all-reduce.14
  1006.7 310.0 all-reduce.12
where the time goes:
time: 1330 us; the launch traced here: 1320 us
  waiting for transfers between devices  927 us (70%)
  blocking collectives  369 us (28%)
  between operations  14.5 us (1%)
    unnamed x6, waiting for transfers between devices  927 us
    all_gather x3, blocking collectives, own_rates(): block_rows = lax.all_gather(deviation, 'src', axis=0, tiled=True)  230 us
    psum x3, blocking collectives, spread(): return lax.psum(block, axis)  139 us
  transfers between devices with their start and end apart: 3, of which 3 were waited for; matrix products, arithmetic and copies ran while one was open for 0% of the time, Pallas kernels for 0%

commit v1 on v0

--- a/solution.py
+++ b/solution.py
@@ -10,7 +10,11 @@
 
 def spread(block, axis, owner):
     block = jnp.where(lax.axis_index(axis) == owner, block, jnp.zeros_like(block))
-    return lax.psum(block, axis)
+
+    def convert_routes_all(block_in, device_axis):
+        return lax.all_gather(block_in, device_axis).sum(axis=0)
+
+    return convert_routes_all(block, device_axis=axis)
 
 
 def kernel_terms(leaves, near_flags, ranks, source):

time: 1330 us -> 1230 us (0.925)
  blocking collectives: 369 us -> 285 us
    psum x3 -> x0, blocking collectives: 139 us -> none  [spread(): return lax.psum(block, axis)]
    all_gather x0 -> x3, blocking collectives: none -> 55.1 us  [convert_routes_all(): return lax.all_gather(block_in, device_axis).sum(axis=0)]
where the time goes in v1:
time: 1230 us
  waiting for transfers between devices  917 us (75%)
  blocking collectives  285 us (23%)
  between operations  14.6 us (1%)
    unnamed x6, waiting for transfers between devices  917 us
    all_gather x3, blocking collectives, own_rates(): block_rows = lax.all_gather(deviation, 'src', axis=0, tiled=True)  230 us
    all_gather x3, blocking collectives, convert_routes_all(): return lax.all_gather(block_in, device_axis).sum(axis=0)  55.1 us
  transfers between devices with their start and end apart: 3, of which 3 were waited for; matrix products, arithmetic and copies ran while one was open for 0% of the time, Pallas kernels for 0%

profile of v1, /device:TPU:8, one launch (start us, length us, event | category | flops | bytes accessed | tf_op | source)
XLA Modules:
  0.0 1231.6 jit_solution(3197148755778227197)
XLA Ops:
  7.2 0.0 all-reduce.17.cloned.1.call-start
  7.3 0.6 copy-done.7
  7.9 0.0 copy-done.2
  8.0 82.7 %all_gather.27 = bf16[256,128]{1,0:T(8,128)(2,1)S(1)} all-gather(bf16[8,128]{1,0:T(8,128)(2,1)S(1)} %get-tuple-element.13), channel_id=1, replica_groups=mesh['tgt'=16,'src'=32] {'src'}, dimensions={0}, use_global_device_ids=true | all-gather | bytes 67584 | tf_op jit(solution)/shard_map/all_gather | solution.py:94
  90.7 0.1 slice.8
  90.8 0.7 copy-done
  91.5 0.1 slice.10
  91.7 18.5 %all-gather = bf16[2048,128]{1,0:T(8,128)(2,1)S(1)} all-gather(bf16[128,128]{1,0:T(8,128)(2,1)S(1)} %dynamic-slice_select_fusion.2), channel_id=2, replica_groups=mesh['tgt'=16,'src'=32] {'tgt'}, dimensions={0}, use_global_device_ids=true | all-gather | bytes 557056 | tf_op jit(solution)/shard_map/all_gather | solution.py:15
  110.2 0.1 reduce_sum.36
  110.2 0.2 fusion.16
  110.5 0.2 fusion.22
  110.7 0.1 copy.20
  110.8 0.1 copy.22
  110.9 0.1 fusion.93
  111.0 0.1 fusion.94
  111.2 0.7 copy-done.8
  111.8 0.1 compare_and_fusion
  111.9 0.9 fusion.1
  112.8 0.9 fusion
  113.6 0.0 all-reduce.17.cloned.1.call-update
  113.7 0.0 all-reduce.15.cloned.1.call-start
  113.7 1.3 dynamic-slice
  115.6 303.1 %all-reduce.17.cloned.1.call-done = (f32[256,128]{1,0:T(8,128)}, f32[256,128]{1,0:T(8,128)}) async-done(((f32[256,128]{1,0:T(8,128)}, f32[256,128]{1,0:T(8,128)}), (f32[256,128]{1,0:T(8,128)}, f32[256,128]{1,0:T(8,128)})) %all-reduce.17.cloned.1.call-update) | async-done | bytes 262160
  418.7 0.7 add_convert_fusion.1
  419.4 73.7 %all_gather.30 = bf16[256,128]{1,0:T(8,128)(2,1)S(1)} all-gather(bf16[8,128]{1,0:T(8,128)(2,1)S(1)} %get-tuple-element.11), channel_id=1, replica_groups=mesh['tgt'=16,'src'=32] {'src'}, dimensions={0}, use_global_device_ids=true | all-gather | bytes 67584 | tf_op jit(solution)/shard_map/all_gather | solution.py:94
  493.1 18.3 %all-gather.1 = bf16[2048,128]{1,0:T(8,128)(2,1)S(1)} all-gather(bf16[128,128]{1,0:T(8,128)(2,1)S(1)} %dynamic-slice_select_fusion.1), channel_id=3, replica_groups=mesh['tgt'=16,'src'=32] {'tgt'}, dimensions={0}, use_global_device_ids=true | all-gather | bytes 557056 | tf_op jit(solution)/shard_map/all_gather | solution.py:15
  511.5 0.1 reduce_sum.37
  511.5 0.1 fusion.95
  511.7 0.1 fusion.96
  511.8 0.2 fusion.14
  512.0 0.2 fusion.20
  512.2 0.9 fusion.3
  513.1 0.9 fusion.2
  514.0 0.0 all-reduce.13.cloned.1.call-start
  514.0 306.9 %all-reduce.15.cloned.1.call-done = (f32[256,128]{1,0:T(8,128)}, f32[256,128]{1,0:T(8,128)}) async-done(((f32[256,128]{1,0:T(8,128)}, f32[256,128]{1,0:T(8,128)}), (f32[256,128]{1,0:T(8,128)}, f32[256,128]{1,0:T(8,128)})) %all-reduce.15.cloned.1.call-update) | async-done | bytes 262160
  820.9 1.3 multiply_add_fusion
  822.3 73.7 %all_gather.33 = bf16[256,128]{1,0:T(8,128)(2,1)S(1)} all-gather(bf16[8,128]{1,0:T(8,128)(2,1)S(1)} %add_convert_fusion), channel_id=1, replica_groups=mesh['tgt'=16,'src'=32] {'src'}, dimensions={0}, use_global_device_ids=true | all-gather | bytes 67584 | tf_op jit(solution)/shard_map/all_gather | solution.py:94
  896.0 18.3 %all-gather.2 = bf16[2048,128]{1,0:T(8,128)(2,1)S(1)} all-gather(bf16[128,128]{1,0:T(8,128)(2,1)S(1)} %dynamic-slice_select_fusion), channel_id=4, replica_groups=mesh['tgt'=16,'src'=32] {'tgt'}, dimensions={0}, use_global_device_ids=true | all-gather | bytes 557056 | tf_op jit(solution)/shard_map/all_gather | solution.py:15
  914.3 0.1 reduce_sum.38
  914.4 0.1 fusion.97
  914.5 0.1 fusion.98
  914.6 0.2 fusion.12
  914.8 0.2 fusion.18
  915.1 0.9 fusion.5
  915.9 0.9 fusion.4
  916.8 0.0 all-reduce.13.cloned.1.call-update
  916.8 306.9 %all-reduce.13.cloned.1.call-done = (f32[256,128]{1,0:T(8,128)}, f32[256,128]{1,0:T(8,128)}) async-done(((f32[256,128]{1,0:T(8,128)}, f32[256,128]{1,0:T(8,128)}), (f32[256,128]{1,0:T(8,128)}, f32[256,128]{1,0:T(8,128)})) %all-reduce.13.cloned.1.call-update) | async-done | bytes 262160
  1223.7 1.4 fusion.71
  (21 shorter events, 0.2 us)
Async XLA Ops:
  7.2 411.5 %all-reduce.17.cloned.1.call-start = ((), (), s32[]{:S(2)}) async-start(), calls=%async_computation.2 | async-start | bytes 524288
  7.2 0.7 copy-start.7
  7.2 0.7 copy-start.2
  7.2 0.7 copy-start.3
  7.2 0.7 copy-start.4
  7.3 0.7 copy-start.5
  7.3 83.4 %copy-start.1 = (bf16[2,1,128,128]{3,2,1,0:T(8,128)(2,1)S(1)}, bf16[2,1,128,128]{3,2,1,0:T(8,128)(2,1)}, u32[]{:S(2)}) copy-start(bf16[2,1,128,128]{3,2,1,0:T(8,128)(2,1)} %param.9) | copy-start | bytes 196612
  90.7 0.8 copy-start
  111.2 0.7 copy-start.8
  113.7 707.3 %all-reduce.15.cloned.1.call-start = ((), (), s32[]{:S(2)}) async-start(), calls=%async_computation.1 | async-start | bytes 524288
  115.6 303.1 %copy-start.6 = (f32[8,128]{1,0:T(8,128)S(1)}, f32[8,128]{1,0:T(8,128)}, u32[]{:S(2)}) copy-start(f32[8,128]{1,0:T(8,128)} %param.17) | copy-start | bytes 12292
  514.0 709.7 %all-reduce.13.cloned.1.call-start = ((), (), s32[]{:S(2)}) async-start(), calls=%async_computation | async-start | bytes 524288
Sparse Core Ops, SparseCore 0:
  113.8 304.8 all-reduce.16
  514.1 306.7 all-reduce.14
  916.9 306.7 all-reduce.12

commit v2 on v0

--- a/solution.py
+++ b/solution.py
@@ -6,6 +6,13 @@
 RMAX = 64
 BLK = 128
 time_step = 0.25
+
+
+def swapped_in(x, mesh_axis, dim):
+    n_dev = lax.axis_size(mesh_axis)
+    blocks = jnp.stack([x for _ in range(n_dev)])
+    blocks = lax.all_to_all(blocks, mesh_axis, split_axis=0, concat_axis=0)
+    return jnp.concatenate(blocks, axis=dim)
 
 
 def spread(block, axis, owner):
@@ -87,7 +94,7 @@
 
     def own_rates(shear_now, normal_now, state_now):
         slip_rate, deviation = friction(shear_now, normal_now, state_now, friction_a)
-        block_rows = lax.all_gather(deviation, "src", axis=0, tiled=True)
+        block_rows = swapped_in(deviation, "src", 0)
         shear_part, normal_part = both_kernels(block_rows)
         shear_rate, normal_rate = (
             lax.psum_scatter(shear_part, "src", scatter_dimension=0, tiled=True),

time: 1330 us -> 1160 us (0.87)
  blocking collectives: 369 us -> 188 us
  starting transfers between devices: 0.12 us -> 18.2 us
    all_gather x3 -> x0, blocking collectives: 230 us -> none  [own_rates(): block_rows = lax.all_gather(deviation, 'src', axis=0, tiled=True)]
    all_to_all x0 -> x2, blocking collectives: none -> 48.8 us  [swapped_in(): blocks = lax.all_to_all(blocks, mesh_axis, split_axis=0, concat_axis=0)]
    all_to_all x0 -> x1, starting transfers between devices: none -> 18.1 us  [swapped_in(): blocks = lax.all_to_all(blocks, mesh_axis, split_axis=0, concat_axis=0)]
    unnamed x6, waiting for transfers between devices: 927 us -> 911 us
  transfers between devices with their start and end apart: 3 -> 4, of which waited for: 3 -> 4; matrix products, arithmetic and copies ran while one was open for 0% -> 0% of each run, Pallas kernels for 0% -> 0%
where the time goes in v2:
time: 1160 us
  waiting for transfers between devices  924 us (80%)
  blocking collectives  188 us (16%)
  starting transfers between devices  18.2 us (2%)
  between operations  14.6 us (1%)
    unnamed x6, waiting for transfers between devices  911 us
    psum x3, blocking collectives, spread(): return lax.psum(block, axis)  139 us
    all_to_all x2, blocking collectives, swapped_in(): blocks = lax.all_to_all(blocks, mesh_axis, split_axis=0, concat_axis=0)  48.8 us
  transfers between devices with their start and end apart: 4, of which 4 were waited for; matrix products, arithmetic and copies ran while one was open for 0% of the time, Pallas kernels for 0%

profile of v2, /device:TPU:8, one launch (start us, length us, event | category | flops | bytes accessed | tf_op | source)
XLA Modules:
  0.0 1160.7 jit_solution(11528724019531364798)
XLA Ops:
  7.2 0.8 add_convert_fusion.2
  7.9 0.6 stack.6
  8.6 18.1 %all-to-all-start = ((bf16[32,8,128]{2,1,0:T(8,128)(2,1)}), bf16[32,8,128]{2,1,0:T(8,128)(2,1)S(1)}, u32[]{:S(2)}, u32[]{:S(2)}) async-start(bf16[32,8,128]{2,1,0:T(8,128)(2,1)} %stack.6), calls=%async_computation | async-start | bytes 131072 | tf_op jit(solution)/shard_map/all_to_all | solution.py:14
  26.7 0.0 all-reduce.17.cloned.1.call-start
  26.8 0.1 slice.8
  26.8 0.0 copy-start
  26.9 0.1 copy.20
  27.0 0.7 copy-done
  27.7 0.1 slice.10
  27.8 0.1 copy.22
  27.9 0.6 copy-done.8
  28.6 0.1 compare_and_fusion
  28.6 13.2 %all-to-all-done = bf16[32,8,128]{2,1,0:T(8,128)(2,1)S(1)} async-done(((bf16[32,8,128]{2,1,0:T(8,128)(2,1)}), bf16[32,8,128]{2,1,0:T(8,128)(2,1)S(1)}, u32[]{:S(2)}, u32[]{:S(2)}) %all-to-all-start) | async-done | bytes 65568 | tf_op jit(solution)/shard_map/all_to_all | solution.py:14
  41.9 47.1 %psum.21 = bf16[128,128]{1,0:T(8,128)(2,1)S(1)} all-reduce(bf16[128,128]{1,0:T(8,128)(2,1)S(1)} %dynamic-slice_select_fusion.2), channel_id=1, replica_groups=mesh['tgt'=16,'src'=32] {'tgt'}, use_global_device_ids=true, to_apply=%region_0.1 | all-reduce | flops 16384 | bytes 65536 | tf_op jit(solution)/shard_map/psum | solution.py:20
  89.0 0.2 fusion.16
  89.2 0.2 fusion.22
  89.4 0.1 fusion.93
  89.5 0.1 fusion.94
  89.6 0.9 fusion.1
  90.5 0.9 fusion
  91.4 0.0 all-reduce.17.cloned.1.call-update
  91.4 0.0 all-reduce.15.cloned.1.call-start
  91.5 1.3 dynamic-slice
  93.5 302.9 %all-reduce.17.cloned.1.call-done = (f32[256,128]{1,0:T(8,128)}, f32[256,128]{1,0:T(8,128)}) async-done(((f32[256,128]{1,0:T(8,128)}, f32[256,128]{1,0:T(8,128)}), (f32[256,128]{1,0:T(8,128)}, f32[256,128]{1,0:T(8,128)})) %all-reduce.17.cloned.1.call-update) | async-done | bytes 262160
  396.4 0.7 add_convert_fusion.1
  397.2 24.4 %all_to_all.15 = bf16[32,8,128]{2,1,0:T(8,128)(2,1)S(1)} all-to-all(bf16[32,8,128]{2,1,0:T(8,128)(2,1)S(1)} %stack.7), channel_id=1, replica_groups=mesh['tgt'=16,'src'=32] {'src'}, dimensions={0} | all-to-all | bytes 131072 | tf_op jit(solution)/shard_map/all_to_all | solution.py:14
  421.6 46.2 %psum.22 = bf16[128,128]{1,0:T(8,128)(2,1)S(1)} all-reduce(bf16[128,128]{1,0:T(8,128)(2,1)S(1)} %dynamic-slice_select_fusion.1), channel_id=1, replica_groups=mesh['tgt'=16,'src'=32] {'tgt'}, use_global_device_ids=true, to_apply=%region_3.4 | all-reduce | flops 16384 | bytes 65536 | tf_op jit(solution)/shard_map/psum | solution.py:20
  467.7 0.1 fusion.95
  467.9 0.1 fusion.96
  468.0 0.2 fusion.14
  468.2 0.2 fusion.20
  468.4 0.9 fusion.3
  469.3 0.9 fusion.2
  470.2 0.0 all-reduce.15.cloned.1.call-update
  470.2 0.0 all-reduce.13.cloned.1.call-start
  470.3 304.1 %all-reduce.15.cloned.1.call-done = (f32[256,128]{1,0:T(8,128)}, f32[256,128]{1,0:T(8,128)}) async-done(((f32[256,128]{1,0:T(8,128)}, f32[256,128]{1,0:T(8,128)}), (f32[256,128]{1,0:T(8,128)}, f32[256,128]{1,0:T(8,128)})) %all-reduce.15.cloned.1.call-update) | async-done | bytes 262160
  774.3 1.3 multiply_add_fusion
  775.7 24.4 %all_to_all.16 = bf16[32,8,128]{2,1,0:T(8,128)(2,1)S(1)} all-to-all(bf16[32,8,128]{2,1,0:T(8,128)(2,1)S(1)} %stack.8), channel_id=1, replica_groups=mesh['tgt'=16,'src'=32] {'src'}, dimensions={0} | all-to-all | bytes 131072 | tf_op jit(solution)/shard_map/all_to_all | solution.py:14
  800.1 46.2 %psum.23 = bf16[128,128]{1,0:T(8,128)(2,1)S(1)} all-reduce(bf16[128,128]{1,0:T(8,128)(2,1)S(1)} %dynamic-slice_select_fusion), channel_id=1, replica_groups=mesh['tgt'=16,'src'=32] {'tgt'}, use_global_device_ids=true, to_apply=%region_6.7 | all-reduce | flops 16384 | bytes 65536 | tf_op jit(solution)/shard_map/psum | solution.py:20
  846.3 0.1 fusion.97
  846.4 0.1 fusion.98
  846.5 0.2 fusion.12
  846.8 0.2 fusion.18
  847.0 0.9 fusion.5
  847.8 0.9 fusion.4
  848.7 0.0 all-reduce.13.cloned.1.call-update
  848.8 304.1 %all-reduce.13.cloned.1.call-done = (f32[256,128]{1,0:T(8,128)}, f32[256,128]{1,0:T(8,128)}) async-done(((f32[256,128]{1,0:T(8,128)}, f32[256,128]{1,0:T(8,128)}), (f32[256,128]{1,0:T(8,128)}, f32[256,128]{1,0:T(8,128)})) %all-reduce.13.cloned.1.call-update) | async-done | bytes 262160
  1152.8 1.3 fusion.71
  (22 shorter events, 0.1 us)
Async XLA Ops:
  8.6 18.1 %copy-start.7 = (s32[2,1]{0,1:T(1,128)S(1)}, s32[2,1]{0,1:T(1,128)}, u32[]{:S(2)}) copy-start(s32[2,1]{0,1:T(1,128)} %param.11) | copy-start | bytes 28
  8.6 18.2 %copy-start.1 = (bf16[2,1,128,128]{3,2,1,0:T(8,128)(2,1)S(1)}, bf16[2,1,128,128]{3,2,1,0:T(8,128)(2,1)}, u32[]{:S(2)}) copy-start(bf16[2,1,128,128]{3,2,1,0:T(8,128)(2,1)} %param.9) | copy-start | bytes 196612
  8.6 33.3 %all-to-all-start = ((bf16[32,8,128]{2,1,0:T(8,128)(2,1)}), bf16[32,8,128]{2,1,0:T(8,128)(2,1)S(1)}, u32[]{:S(2)}, u32[]{:S(2)}) async-start(bf16[32,8,128]{2,1,0:T(8,128)(2,1)} %stack.6), calls=%async_computation | async-start | bytes 131072 | tf_op jit(solution)/shard_map/all_to_all | solution.py:14
  26.7 369.7 %all-reduce.17.cloned.1.call-start = ((), (), s32[]{:S(2)}) async-start(), calls=%async_computation.5 | async-start | bytes 524288
  26.8 0.8 copy-start
  27.9 0.7 copy-start.8
  91.4 305.0 %copy-start.5 = (f32[8,128]{1,0:T(8,128)S(1)}, f32[8,128]{1,0:T(8,128)}, u32[]{:S(2)}) copy-start(f32[8,128]{1,0:T(8,128)} %param.15) | copy-start | bytes 12292
  91.4 305.0 %copy-start.6 = (f32[8,128]{1,0:T(8,128)S(1)}, f32[8,128]{1,0:T(8,128)}, u32[]{:S(2)}) copy-start(f32[8,128]{1,0:T(8,128)} %param.17) | copy-start | bytes 12292
  91.4 682.9 %all-reduce.15.cloned.1.call-start = ((), (), s32[]{:S(2)}) async-start(), calls=%async_computation.4 | async-start | bytes 524288
  92.8 303.6 %copy-start.4 = (f32[8,128]{1,0:T(8,128)S(1)}, f32[8,128]{1,0:T(8,128)}, u32[]{:S(2)}) copy-start(f32[8,128]{1,0:T(8,128)} %param.16) | copy-start | bytes 12292
  92.8 303.6 %copy-start.3 = (f32[8,128]{1,0:T(8,128)S(1)}, f32[8,128]{1,0:T(8,128)}, u32[]{:S(2)}) copy-start(f32[8,128]{1,0:T(8,128)} %param.14) | copy-start | bytes 12292
  93.4 303.0 %copy-start.2 = (f32[8,128]{1,0:T(8,128)S(1)}, f32[8,128]{1,0:T(8,128)}, u32[]{:S(2)}) copy-start(f32[8,128]{1,0:T(8,128)} %param.13) | copy-start | bytes 12292
  470.2 682.6 %all-reduce.13.cloned.1.call-start = ((), (), s32[]{:S(2)}) async-start(), calls=%async_computation.3 | async-start | bytes 524288
Sparse Core Ops, SparseCore 0:
  91.6 304.7 all-reduce.16
  470.3 303.9 all-reduce.14
  848.9 303.9 all-reduce.12
